TPU v7x, 32 devices: a whole 2x2x4 slice. The times are simulated.
32 devices in a mesh: groups: 2 (over x), hits: 8 (over z, y), heads: 2 (over core).
Axes of the slice: x: 2, y: 2, z: 4, core: 2. Of those that a mesh axis runs over, the one named last changes fastest.
Arguments:
- queries: bfloat16 [2048, 2048], P('groups', 'heads'), parts along dimension 0, may hold values from -13.5 to 13.5
- keys: bfloat16 [8192, 2048], P(('groups', 'hits'), 'heads'), parts along dimension 0, may hold values from -36 to 36
- values: bfloat16 [8192, 2048], P(('groups', 'hits'), 'heads'), parts along dimension 0, may hold values from -6 to 6
- hit_counts: int32 [16], P(('groups', 'hits')), parts along dimension 0, may hold values from 128 to 512, as said below
- latents: bfloat16 [2048, 2048], P(('groups', 'hits'), 'heads'), parts along dimension 0, may hold values from -23 to 23
- out_proj: bfloat16 [2048, 2048], P('heads'), may hold values from -1 to 1
- norm_gain: float32 [2048], P('heads'), may hold values from 0.1 to 1.9
- up_proj: bfloat16 [2048, 8192], P('heads', 'hits'), may hold values from -0.125 to 0.125
- down_proj: bfloat16 [8192, 2048], P('hits', 'heads'), may hold values from -0.25 to 0.25
Outputs:
- mixed: bfloat16 [2048, 2048], P(('groups', 'hits'), 'heads'), parts along dimension 0
There are 2 independent parts, one for each index of `groups`. A program takes and returns all parts, laid end to end along the dimension named above; an argument that names none is the same for every part. Nothing has to cross between parts.
Inputs may be any that keep to these rules, and one draw needn't show every extreme that they name: hit_counts[s] live hits fill the first slots of shard s; some shard is full and some holds exactly 128.
All inputs are finite; a program needn't handle non-finite values.
Results may differ from a plain program's by a relative error of at most 0.012.
Values may be sent and summed in bfloat16 or wider, within the bound.
No kernel may reach another device: no remote copies, remote signals or barrier semaphores. Data moves between devices by JAX's collectives and lax.ppermute only.
A program may use at most 64 MiB of HBM per device.

v0:
```python
import math
import jax
import jax.numpy as jnp
from jax import lax
from jax.sharding import PartitionSpec as P

D = 2048
HD = 128


def shards(queries, keys, values, hit_counts, latents, out_proj, norm_gain, up_proj, down_proj):
    width = keys.shape[1]
    local_heads = width // HD
    score_scale = 1.0 / math.sqrt(HD)
    live_mask = lax.broadcasted_iota(jnp.int32, (1, keys.shape[0]), 1) < hit_counts[0]

    def merged(row_top, row_total, context):
        row_best = lax.pmax(row_top, "hits")
        factor = jnp.exp(row_top - row_best)
        total_sum, context_sum = (
            lax.psum_scatter(row_total * factor, "hits", scatter_dimension=1, tiled=True),
            lax.psum_scatter(context * factor[..., None], "hits", scatter_dimension=1, tiled=True),
        )
        return (context_sum / total_sum[..., None]).astype(jnp.bfloat16)

    def one_head(head_index):
        col_start = head_index * HD
        q_head = lax.dynamic_slice_in_dim(queries, col_start, HD, 1)
        k_head = lax.dynamic_slice_in_dim(keys, col_start, HD, 1)
        v_head = lax.dynamic_slice_in_dim(values, col_start, HD, 1)
        scores = (
            lax.dot_general(
                q_head, k_head, (((1,), (1,)), ((), ())), preferred_element_type=jnp.float32
            )
            * score_scale
        )
        scores = jnp.where(live_mask, scores, -1e30)
        row_top = jnp.max(scores, axis=1)
        weights = jnp.where(live_mask, jnp.exp(scores - row_top[:, None]), 0.0)
        row_total = jnp.sum(weights, axis=1)
        context = jnp.dot(weights.astype(jnp.bfloat16), v_head, preferred_element_type=jnp.float32)
        return (row_top, row_total, context)

    context = merged(*lax.map(one_head, jnp.arange(local_heads, dtype=jnp.int32)))
    weights_out = out_proj.reshape(local_heads, HD, out_proj.shape[1])
    projected = jnp.einsum("hrd,hde->re", context, weights_out, preferred_element_type=jnp.float32)
    attended = lax.psum_scatter(projected, "heads", scatter_dimension=1, tiled=True)
    stream = latents.astype(jnp.float32) + attended
    squares = lax.psum(jnp.sum(stream * stream, axis=1), "heads")
    normed = (stream * lax.rsqrt(squares / D + 1e-06)[:, None] * norm_gain[None, :]).astype(
        jnp.bfloat16
    )
    partial_units = jnp.dot(
        lax.all_gather(normed, "hits", axis=0, tiled=True),
        up_proj,
        preferred_element_type=jnp.float32,
    )
    summed_units = lax.psum(partial_units, "heads")
    hidden = jax.nn.gelu(summed_units).astype(jnp.bfloat16)
    branch_out = lax.psum_scatter(
        jnp.dot(hidden, down_proj, preferred_element_type=jnp.float32),
        "hits",
        scatter_dimension=0,
        tiled=True,
    )
    return (stream + branch_out).astype(jnp.bfloat16)


def solution(mesh):
    return jax.shard_map(
        shards,
        mesh=mesh,
        in_specs=(
            P("groups", "heads"),
            P(("groups", "hits"), "heads"),
            P(("groups", "hits"), "heads"),
            P(("groups", "hits")),
            P(("groups", "hits"), "heads"),
            P("heads", None),
            P("heads"),
            P("heads", "hits"),
            P("hits", "heads"),
        ),
        out_specs=P(("groups", "hits"), "heads"),
        check_vma=False,
    )
```

profile of v0, /device:TPU:0, one launch (start us, length us, event | category | flops | bytes accessed | tf_op | source)
XLA Modules:
  0.0 451.4 jit_solution(14915383482989247984)
XLA Ops:
  6.5 54.9 %while.15 = (s32[]{:T(128)}, f32[8,1024]{1,0:T(8,128)S(1)}, f32[8,1024]{1,0:T(8,128)S(1)}, f32[8,1024,128]{2,1,0:T(8,128)}, s32[8]{0:T(128)S(1)}, /*index=5*/bf1...) while((s32[]{:T(128)}, f32[8,1024]{1,0:T(8,128)S(1)}, ...), condition=%wide.region_3.4_spmd.clone, body=%wide.region_0.3_spmd.clone.sunk | while | flops 275249664 | bytes 7376583 | solution.py:44
  8.6 1.4 fusion.52
  10.1 2.5 fusion.54
  15.4 1.4 fusion.52
  16.9 2.6 fusion.54
  22.3 1.4 fusion.52
  23.8 2.6 fusion.54
  29.2 1.4 fusion.52
  30.6 2.6 fusion.54
  36.0 1.4 fusion.52
  37.5 2.6 fusion.54
  42.9 1.4 fusion.52
  44.4 2.6 fusion.54
  49.8 1.5 fusion.52
  51.2 2.5 fusion.54
  56.6 1.4 fusion.52
  58.1 2.6 fusion.54
  61.5 38.9 %pmax.7 = f32[8,1024]{1,0:T(8,128)S(1)} all-reduce(f32[8,1024]{1,0:T(8,128)S(1)} %get-tuple-element.55), channel_id=1, replica_groups=mesh['groups'=2,'hits'=8,'heads'=2] {'hits'}, use_global_device_ids=true, to_apply=%region_4.5 | all-reduce | flops 8192 | bytes 65536 | tf_op jit(solution)/shard_map/pmax | solution.py:18
  101.0 4.2 broadcast_multiply_fusion
  105.3 47.9 %reduce-scatter.7.cloned.1.call-done = f32[8,128]{1,0:T(8,128)} async-done(((f32[8,1024]{1,0:T(8,128)}), f32[8,128]{1,0:T(8,128)}) %reduce-scatter.7.cloned.1.call-update) | async-done | bytes 4112 | tf_op jit(solution)/shard_map/reduce_scatter | solution.py:21
  153.2 91.0 %reduce-scatter.5.cloned.1.call-done = f32[8,128,128]{2,1,0:T(8,128)} async-done(((f32[8,1024,128]{2,1,0:T(8,128)}), f32[8,128,128]{2,1,0:T(8,128)}) %reduce-scatter.5.cloned.1.call-update) | async-done | bytes 524304 | tf_op jit(solution)/shard_map/reduce_scatter | solution.py:22
  244.2 4.2 convolution_bitcast_fusion.1
  248.4 8.1 %reduce-scatter.9.cloned.1.call-done = f32[128,1024]{1,0:T(8,128)} async-done(((f32[128,2048]{1,0:T(8,128)}), f32[128,1024]{1,0:T(8,128)}) %reduce-scatter.9.cloned.1.call-update) | async-done | bytes 524304 | tf_op jit(solution)/shard_map/reduce_scatter | solution.py:47
  256.5 1.2 multiply_reduce_fusion
  257.7 2.5 psum.14
  260.2 1.9 multiply_convert_fusion
  262.1 50.4 %all-gather.2.cloned.1.call-done = bf16[1024,1024]{1,0:T(8,128)(2,1)} async-done(((bf16[128,1024]{1,0:T(8,128)(2,1)}), bf16[1024,1024]{1,0:T(8,128)(2,1)}) %all-gather.2.cloned.1.call-update) | async-done | bytes 2097168 | tf_op jit(solution)/shard_map/all_gather | solution.py:54
  312.5 5.9 %fusion.40 = f32[1024,1024]{1,0:T(8,128)} fusion(bf16[1024,1024]{1,0:T(8,128)(2,1)} %all-gather.2.cloned.1.call-done, bf16[1024,1024]{1,0:T(8,128)(2,1)S(1)} %copy-done), kind=kOutput, calls=%fused_computation.51 | convolution fusion | flops 2147483648 | bytes 8388608 | tf_op jit(solution)/shard_map/dot_general | solution.py:53
  318.5 26.7 %all-reduce.2.cloned.1.call-done = f32[1024,1024]{1,0:T(8,128)} async-done(((f32[1024,1024]{1,0:T(8,128)}), f32[1024,1024]{1,0:T(8,128)}) %all-reduce.2.cloned.1.call-update) | async-done | bytes 4194320 | tf_op jit(solution)/shard_map/psum | solution.py:58
  345.2 7.5 %fusion.28 = f32[1024,1024]{1,0:T(8,128)} fusion(bf16[1024,1024]{1,0:T(8,128)(2,1)} %param.19, f32[1024,1024]{1,0:T(8,128)} %all-reduce.2.cloned.1.call-done), kind=kOutput, calls=%fused_computation.32 | convolution fusion | flops 2156920832 | bytes 10485760 | tf_op jit(solution)/shard_map/dot_general | solution.py:61
  352.7 90.0 %reduce-scatter.11.cloned.1.call-done = f32[128,1024]{1,0:T(8,128)} async-done(((f32[1024,1024]{1,0:T(8,128)}), f32[128,1024]{1,0:T(8,128)}) %reduce-scatter.11.cloned.1.call-update) | async-done | bytes 524304 | tf_op jit(solution)/shard_map/reduce_scatter | solution.py:60
  442.8 1.8 add_convert_fusion
  (66 shorter events, 17.9 us)
Async XLA Ops:
  6.5 306.0 %copy-start = (bf16[1024,1024]{1,0:T(8,128)(2,1)S(1)}, bf16[1024,1024]{1,0:T(8,128)(2,1)}, u32[]{:S(2)}) copy-start(bf16[1024,1024]{1,0:T(8,128)(2,1)} %param.18) | copy-start | bytes 6291460
  6.5 146.6 %reduce-scatter.7.cloned.1.call-start = ((), (), s32[]{:S(2)}) async-start(), calls=%async_computation.5 | async-start | bytes 36864 | tf_op jit(solution)/shard_map/reduce_scatter | solution.py:21
  101.0 143.2 %reduce-scatter.5.cloned.1.call-start = ((), (), s32[]{:S(2)}) async-start(), calls=%async_computation.4 | async-start | bytes 4718592 | tf_op jit(solution)/shard_map/reduce_scatter | solution.py:22
  105.3 151.3 %reduce-scatter.9.cloned.1.call-start = ((), (), s32[]{:S(2)}) async-start(), calls=%async_computation.6 | async-start | bytes 1572864 | tf_op jit(solution)/shard_map/reduce_scatter | solution.py:47
  244.2 12.4 %copy-start.2 = (bf16[128,1024]{1,0:T(8,128)(2,1)S(1)}, bf16[128,1024]{1,0:T(8,128)(2,1)}, u32[]{:S(2)}) copy-start(bf16[128,1024]{1,0:T(8,128)(2,1)} %param.15) | copy-start | bytes 786436
  244.2 16.0 %copy-start.3 = (f32[1024]{0:T(1024)S(1)}, f32[1024]{0:T(1024)}, u32[]{:S(2)}) copy-start(f32[1024]{0:T(1024)} %param.17) | copy-start | bytes 12292
  248.4 64.2 %all-gather.2.cloned.1.call-start = ((), (), s32[]{:S(2)}) async-start(), calls=%async_computation.7 | async-start | bytes 2359296 | tf_op jit(solution)/shard_map/all_gather | solution.py:54
  262.1 83.1 %all-reduce.2.cloned.1.call-start = ((), (), s32[]{:S(2)}) async-start(), calls=%async_computation.8 | async-start | bytes 8388608 | tf_op jit(solution)/shard_map/psum | solution.py:58
  318.5 124.3 %reduce-scatter.11.cloned.1.call-start = ((), (), s32[]{:S(2)}) async-start(), calls=%async_computation.9 | async-start | bytes 4718592 | tf_op jit(solution)/shard_map/reduce_scatter | solution.py:60
  352.7 90.1 %copy-start.1 = (f32[128,1024]{1,0:T(8,128)S(1)}, f32[128,1024]{1,0:T(8,128)}, u32[]{:S(2)}) copy-start(f32[128,1024]{1,0:T(8,128)} %reduce-scatter.9.cloned.1.call-done) | copy-start | bytes 1572868
Sparse Core Ops, SparseCore 0:
  101.1 52.0 reduce-scatter.6
  156.8 87.3 reduce-scatter.4
  248.5 8.0 reduce-scatter.8
  262.2 50.2 all-gather.1
  318.6 26.6 all-reduce.1
  352.9 89.8 reduce-scatter.10
where the time goes:
time: 452 us; the launch traced here: 451 us
  waiting for transfers between devices  314 us (69%)
  matrix products  49.5 us (11%)
  blocking collectives  41.3 us (9%)
  other arithmetic  19.6 us (4%)
  between operations  13.5 us (3%)
  local copies, waits for them, and re-layouts  7.08 us (2%)
  loops' own time  5.98 us (1%)
    reduce_scatter x1, waiting for transfers between devices, merged(): lax.psum_scatter(context * factor[..., None], 'hits', scatter_dimension=1...  91 us
    reduce_scatter x1, waiting for transfers between devices, shards(): lax.psum_scatter(jnp.dot(hidden, down_proj, preferred_element_type=jnp.fl...  90 us
    all_gather x1, waiting for transfers between devices, shards(): lax.all_gather(normed, 'hits', axis=0, tiled=True)  50.4 us
    reduce_scatter x1, waiting for transfers between devices, merged(): lax.psum_scatter(row_total * factor, 'hits', scatter_dimension=1, tiled=T...  47.9 us
    pmax x1, blocking collectives, merged(): row_best = lax.pmax(row_top, 'hits')  38.9 us
    psum x1, waiting for transfers between devices, shards(): summed_units = lax.psum(partial_units, 'heads')  26.7 us
    dot_general x8, matrix products, one_head(): jnp.dot(weights.astype(jnp.bfloat16), v_head, preferred_element_type=jnp....  20.5 us
    dot_general x8, matrix products, one_head(): lax.dot_general(q_head, k_head, (((1,), (1,)), ((), ())), preferred_eleme...  11.6 us
  transfers between devices with their start and end apart: 6, of which 6 were waited for; matrix products, arithmetic and copies ran while one was open for 1% of the time, Pallas kernels for 0%

commit v1 on v0

--- a/solution.py
+++ b/solution.py
@@ -50,10 +50,22 @@
     normed = (stream * lax.rsqrt(squares / D + 1e-06)[:, None] * norm_gain[None, :]).astype(
         jnp.bfloat16
     )
+
+    def direct_the_words(block_in, peer_axis, array_axis):
+        row_out = lax.axis_size(peer_axis)
+        t1 = lax.axis_index(peer_axis)
+        arr_now, outer, block_last = (row_out, t1, block_in.shape[array_axis])
+        out_arr, current_block = (block_in, 1)
+        while current_block < arr_now:
+            part_now = lax.ppermute(
+                out_arr, peer_axis, [(u, (u - current_block) % arr_now) for u in range(arr_now)]
+            )
+            out_arr = jnp.concatenate([out_arr, part_now], array_axis)
+            current_block = 2 * current_block
+        return jnp.roll(out_arr, outer * block_last, axis=array_axis)
+
     partial_units = jnp.dot(
-        lax.all_gather(normed, "hits", axis=0, tiled=True),
-        up_proj,
-        preferred_element_type=jnp.float32,
+        direct_the_words(normed, "hits", 0), up_proj, preferred_element_type=jnp.float32
     )
     summed_units = lax.psum(partial_units, "heads")
     hidden = jax.nn.gelu(summed_units).astype(jnp.bfloat16)

time: 452 us -> 484 us (1.071)
  waiting for transfers between devices: 314 us -> 330 us
  local copies, waits for them, and re-layouts: 7.08 us -> 15.6 us
  starting transfers between devices: 0.21 us -> 7.04 us
    ppermute x0 -> x3, waiting for transfers between devices: none -> 62.7 us  [direct_the_words(): lax.ppermute(out_arr, peer_axis, [(u, (u - current_block) % arr_now) for...]
    all_gather x1 -> x0, waiting for transfers between devices: 50.4 us -> none  [shards(): lax.all_gather(normed, 'hits', axis=0, tiled=True)]
    ppermute x0 -> x3, starting transfers between devices: none -> 6.87 us  [direct_the_words(): lax.ppermute(out_arr, peer_axis, [(u, (u - current_block) % arr_now) for...]
    unnamed x8 -> x14, local copies, waits for them, and re-layouts: 0.02 us -> 6.22 us
  transfers between devices with their start and end apart: 6 -> 8, of which waited for: 6 -> 8; matrix products, arithmetic and copies ran while one was open for 1% -> 1% of each run, Pallas kernels for 0% -> 0%
where the time goes in v1:
time: 484 us; the launch traced here: 483 us
  waiting for transfers between devices  330 us (68%)
  matrix products  49.5 us (10%)
  blocking collectives  41.3 us (9%)
  other arithmetic  20.7 us (4%)
  local copies, waits for them, and re-layouts  15.6 us (3%)
  between operations  13.2 us (3%)
  starting transfers between devices  7.04 us (1%)
  loops' own time  5.98 us (1%)
    reduce_scatter x1, waiting for transfers between devices, merged(): lax.psum_scatter(context * factor[..., None], 'hits', scatter_dimension=1...  91 us
    reduce_scatter x1, waiting for transfers between devices, shards(): lax.psum_scatter(jnp.dot(hidden, down_proj, preferred_element_type=jnp.fl...  90.1 us
    ppermute x3, waiting for transfers between devices, direct_the_words(): lax.ppermute(out_arr, peer_axis, [(u, (u - current_block) % arr_now) for...  62.7 us
    reduce_scatter x1, waiting for transfers between devices, merged(): lax.psum_scatter(row_total * factor, 'hits', scatter_dimension=1, tiled=T...  47.8 us
    pmax x1, blocking collectives, merged(): row_best = lax.pmax(row_top, 'hits')  38.9 us
    psum x1, waiting for transfers between devices, shards(): summed_units = lax.psum(partial_units, 'heads')  30.1 us
    dot_general x8, matrix products, one_head(): jnp.dot(weights.astype(jnp.bfloat16), v_head, preferred_element_type=jnp....  20.5 us
    dot_general x8, matrix products, one_head(): lax.dot_general(q_head, k_head, (((1,), (1,)), ((), ())), preferred_eleme...  11.6 us
  transfers between devices with their start and end apart: 8, of which 8 were waited for; matrix products, arithmetic and copies ran while one was open for 1% of the time, Pallas kernels for 0%

profile of v1, /device:TPU:0, one launch (start us, length us, event | category | flops | bytes accessed | tf_op | source)
XLA Modules:
  0.0 483.2 jit_solution(7576463780497924961)
XLA Ops:
  6.5 54.9 %while.15 = (s32[]{:T(128)}, f32[8,1024]{1,0:T(8,128)S(1)}, f32[8,1024]{1,0:T(8,128)S(1)}, f32[8,1024,128]{2,1,0:T(8,128)}, s32[8]{0:T(128)S(1)}, /*index=5*/bf1...) while((s32[]{:T(128)}, f32[8,1024]{1,0:T(8,128)S(1)}, ...), condition=%wide.region_3.4_spmd.clone, body=%wide.region_0.3_spmd.clone.sunk | while | flops 275249664 | bytes 7376583 | solution.py:44
  8.6 1.4 fusion.53
  10.1 2.5 fusion.55
  16.9 2.6 fusion.55
  23.8 2.6 fusion.55
  30.6 2.6 fusion.55
  37.5 2.6 fusion.55
  44.4 2.6 fusion.55
  49.8 1.5 fusion.53
  51.2 2.5 fusion.55
  56.6 1.4 fusion.53
  58.1 2.6 fusion.55
  61.5 38.9 %pmax.7 = f32[8,1024]{1,0:T(8,128)S(1)} all-reduce(f32[8,1024]{1,0:T(8,128)S(1)} %get-tuple-element.55), channel_id=1, replica_groups=mesh['groups'=2,'hits'=8,'heads'=2] {'hits'}, use_global_device_ids=true, to_apply=%region_4.5 | all-reduce | flops 8192 | bytes 65536 | tf_op jit(solution)/shard_map/pmax | solution.py:18
  101.0 4.2 broadcast_multiply_fusion
  105.3 47.8 %reduce-scatter.7.cloned.1.call-done = f32[8,128]{1,0:T(8,128)} async-done(((f32[8,1024]{1,0:T(8,128)}), f32[8,128]{1,0:T(8,128)}) %reduce-scatter.7.cloned.1.call-update) | async-done | bytes 4112 | tf_op jit(solution)/shard_map/reduce_scatter | solution.py:21
  153.2 91.0 %reduce-scatter.5.cloned.1.call-done = f32[8,128,128]{2,1,0:T(8,128)} async-done(((f32[8,1024,128]{2,1,0:T(8,128)}), f32[8,128,128]{2,1,0:T(8,128)}) %reduce-scatter.5.cloned.1.call-update) | async-done | bytes 524304 | tf_op jit(solution)/shard_map/reduce_scatter | solution.py:22
  244.2 4.1 convolution_bitcast_fusion.1
  248.4 8.1 %reduce-scatter.9.cloned.1.call-done = f32[128,1024]{1,0:T(8,128)} async-done(((f32[128,2048]{1,0:T(8,128)}), f32[128,1024]{1,0:T(8,128)}) %reduce-scatter.9.cloned.1.call-update) | async-done | bytes 524304 | tf_op jit(solution)/shard_map/reduce_scatter | solution.py:47
  257.7 2.5 psum.14
  260.2 1.9 constant_dynamic-update-slice_fusion.7
  262.0 4.5 collective-permute-start
  266.6 6.0 %collective-permute-done = bf16[128,1024]{1,0:T(8,128)(2,1)S(1)} collective-permute-done((bf16[128,1024]{1,0:T(8,128)(2,1)S(1)}, bf16[128,1024]{1,0:T(8,128)(2,1)S(1)}, u32[]{:S(2)}, u32[]{:S(2)}) %collective-permute-start) | collective-permute-done | bytes 262176 | tf_op jit(solution)/shard_map/ppermute | solution.py:60
  272.6 1.6 collective-permute-start.1
  274.2 11.7 %collective-permute-done.1 = bf16[256,1024]{1,0:T(8,128)(2,1)S(1)} collective-permute-done((bf16[256,1024]{1,0:T(8,128)(2,1)S(1)}, bf16[256,1024]{1,0:T(8,128)(2,1)S(1)}, u32[]{:S(2)}, u32[]{:S(2)}) %collective-permute-start.1) | collective-permute-done | bytes 524320 | tf_op jit(solution)/shard_map/ppermute | solution.py:60
  289.2 45.0 %collective-permute-done.2 = bf16[512,1024]{1,0:T(8,128)(2,1)} collective-permute-done((bf16[512,1024]{1,0:T(8,128)(2,1)}, bf16[512,1024]{1,0:T(8,128)(2,1)}, u32[]{:S(2)}, u32[]{:S(2)}) %collective-permute-start.2) | collective-permute-done | bytes 1048608 | tf_op jit(solution)/shard_map/ppermute | solution.py:60
  334.3 2.3 constant_dynamic-update-slice_fusion.4
  338.9 2.3 constant_dynamic-update-slice_fusion
  341.2 5.9 %fusion.34 = f32[1024,1024]{1,0:T(8,128)} fusion(bf16[1024,1024]{1,0:T(8,128)(2,1)S(1)} %copy-done, bf16[2048,1024]{1,0:T(8,128)(2,1)} %constant_dynamic-update-slice_fusion, s32[]{:T(128)S(6)} %select_n.26), kind=kOutput, calls=%fused_computation.37 | convolution fusion | flops 2147483648 | bytes 8388612 | tf_op jit(solution)/shard_map/dot_general | solution.py:67
  347.1 30.1 %all-reduce.2.cloned.1.call-done = f32[1024,1024]{1,0:T(8,128)} async-done(((f32[1024,1024]{1,0:T(8,128)}), f32[1024,1024]{1,0:T(8,128)}) %all-reduce.2.cloned.1.call-update) | async-done | bytes 4194320 | tf_op jit(solution)/shard_map/psum | solution.py:70
  377.2 7.5 %fusion.28 = f32[1024,1024]{1,0:T(8,128)} fusion(bf16[1024,1024]{1,0:T(8,128)(2,1)} %param.19, f32[1024,1024]{1,0:T(8,128)} %all-reduce.2.cloned.1.call-done), kind=kOutput, calls=%fused_computation.32 | convolution fusion | flops 2156920832 | bytes 10485760 | tf_op jit(solution)/shard_map/dot_general | solution.py:73
  384.7 90.1 %reduce-scatter.11.cloned.1.call-done = f32[128,1024]{1,0:T(8,128)} async-done(((f32[1024,1024]{1,0:T(8,128)}), f32[128,1024]{1,0:T(8,128)}) %reduce-scatter.11.cloned.1.call-update) | async-done | bytes 524304 | tf_op jit(solution)/shard_map/reduce_scatter | solution.py:72
  474.8 1.8 add_convert_fusion
  (78 shorter events, 31.9 us)
Async XLA Ops:
  6.5 334.6 %copy-start = (bf16[1024,1024]{1,0:T(8,128)(2,1)S(1)}, bf16[1024,1024]{1,0:T(8,128)(2,1)}, u32[]{:S(2)}) copy-start(bf16[1024,1024]{1,0:T(8,128)(2,1)} %param.18) | copy-start | bytes 6291460
  6.5 146.6 %reduce-scatter.7.cloned.1.call-start = ((), (), s32[]{:S(2)}) async-start(), calls=%async_computation.5 | async-start | bytes 36864 | tf_op jit(solution)/shard_map/reduce_scatter | solution.py:21
  101.0 143.2 %reduce-scatter.5.cloned.1.call-start = ((), (), s32[]{:S(2)}) async-start(), calls=%async_computation.4 | async-start | bytes 4718592 | tf_op jit(solution)/shard_map/reduce_scatter | solution.py:22
  105.3 151.3 %copy-start.2 = (bf16[128,1024]{1,0:T(8,128)(2,1)S(1)}, bf16[128,1024]{1,0:T(8,128)(2,1)}, u32[]{:S(2)}) copy-start(bf16[128,1024]{1,0:T(8,128)(2,1)} %param.15) | copy-start | bytes 786436
  105.3 154.9 %copy-start.3 = (f32[1024]{0:T(1024)S(1)}, f32[1024]{0:T(1024)}, u32[]{:S(2)}) copy-start(f32[1024]{0:T(1024)} %param.17) | copy-start | bytes 12292
  105.3 151.2 %reduce-scatter.9.cloned.1.call-start = ((), (), s32[]{:S(2)}) async-start(), calls=%async_computation.6 | async-start | bytes 1572864 | tf_op jit(solution)/shard_map/reduce_scatter | solution.py:47
  248.3 128.9 %all-reduce.2.cloned.1.call-start = ((), (), s32[]{:S(2)}) async-start(), calls=%async_computation.7 | async-start | bytes 8388608 | tf_op jit(solution)/shard_map/psum | solution.py:70
  262.0 10.5 %collective-permute-start = (bf16[128,1024]{1,0:T(8,128)(2,1)S(1)}, bf16[128,1024]{1,0:T(8,128)(2,1)S(1)}, u32[]{:S(2)}, u32[]{:S(2)}) collective-permute-start(bf16[128,1024]{1,0:T(8,128)(2,1)S(1)} %get-tuple-element.97), channel_id=1, source_target_pairs={{0,14},{2,0},{4,2},{6,4},{8,6},{10,8},{12,10},{14,12},{1,15},{3,1}... | collective-permute-start | bytes 786440 | tf_op jit(solution)/shard_map/ppermute | solution.py:60
  272.6 13.3 %collective-permute-start.1 = (bf16[256,1024]{1,0:T(8,128)(2,1)S(1)}, bf16[256,1024]{1,0:T(8,128)(2,1)S(1)}, u32[]{:S(2)}, u32[]{:S(2)}) collective-permute-start(bf16[256,1024]{1,0:T(8,128)(2,1)S(1)} %pad_maximum_fusion.1), channel_id=1, source_target_pairs={{0,12},{2,14},{4,0},{6,2},{8,4},{10,6},{12,8},{14,10},{1,13},{3,15... | collective-permute-start | bytes 1572872 | tf_op jit(solution)/shard_map/ppermute | solution.py:60
  287.0 47.3 %collective-permute-start.2 = (bf16[512,1024]{1,0:T(8,128)(2,1)}, bf16[512,1024]{1,0:T(8,128)(2,1)}, u32[]{:S(2)}, u32[]{:S(2)}) collective-permute-start(bf16[512,1024]{1,0:T(8,128)(2,1)} %pad_maximum_fusion), channel_id=1, source_target_pairs={{0,8},{2,10},{4,12},{6,14},{8,0},{10,2},{12,4},{14,6},{1,9},{3,11}... | collective-permute-start | bytes 3145736 | tf_op jit(solution)/shard_map/ppermute | solution.py:60
  347.1 127.7 %reduce-scatter.11.cloned.1.call-start = ((), (), s32[]{:S(2)}) async-start(), calls=%async_computation.8 | async-start | bytes 4718592 | tf_op jit(solution)/shard_map/reduce_scatter | solution.py:72
  384.7 90.1 %copy-start.1 = (f32[128,1024]{1,0:T(8,128)S(1)}, f32[128,1024]{1,0:T(8,128)}, u32[]{:S(2)}) copy-start(f32[128,1024]{1,0:T(8,128)} %reduce-scatter.9.cloned.1.call-done) | copy-start | bytes 1572868
Sparse Core Ops, SparseCore 0:
  101.1 52.0 reduce-scatter.6
  156.8 87.3 reduce-scatter.4
  248.4 8.0 reduce-scatter.8
  347.2 29.9 all-reduce.1
  384.8 89.9 reduce-scatter.10
